TPU v7x, 128 devices: a whole 4x4x4 slice. The times are simulated.
128 devices in a mesh: seq: 4 (over z_lo, core), res: 32 (over y, x, z_hi).
Axes of the slice: x: 4, y: 4, z: 4 (z_hi: 2, z_lo: 2; z = z_hi * 2 + z_lo), core: 2. Of those that a mesh axis runs over, the one named last changes fastest.
Arguments:
- homolog_embedding: bfloat16 [16, 2048, 256], P('seq', 'res'), may hold values from -6 to 6
- pair_input_rows: bfloat16 [2048, 2048, 128], P('res', 'seq'), may hold values from -256 to 256
- incoming_slope: bfloat16 [16, 2048, 256], P('seq', 'res'), may hold values from -6 to 6
- rescale_factor: float32 [256], replicated, may hold values from 0.25 to 1.75
- probe_weights: bfloat16 [256, 256], replicated, may hold values from -0.375 to 0.375
- lookup_weights: bfloat16 [256, 256], replicated, may hold values from -0.375 to 0.375
- content_weights: bfloat16 [256, 256], replicated, may hold values from -0.375 to 0.375
- sigmoid_weights: bfloat16 [256, 256], replicated, may hold values from -0.375 to 0.375
- final_projection: bfloat16 [256, 256], replicated, may hold values from -0.375 to 0.375
- pair_bias_matrix: bfloat16 [128, 8], replicated, may hold values from -1 to 1
Outputs:
- alignment_rows_gradient: bfloat16 [16, 2048, 256], P('seq', 'res')
- pair_input_gradient: bfloat16 [2048, 2048, 128], P('res', 'seq')
- layer_gain_gradient: float32 [256], replicated
- query_matrix_gradient: float32 [256, 256], replicated
- key_matrix_gradient: float32 [256, 256], replicated
- value_matrix_gradient: float32 [256, 256], replicated
- gate_matrix_gradient: float32 [256, 256], replicated
- final_projection_slope: float32 [256, 256], replicated
- pair_bias_matrix_gradient: float32 [128, 8], replicated
All inputs are finite; a program needn't handle non-finite values.
Results may differ from a plain program's by a relative error of at most 0.0034.
The roundings to bfloat16 on the way count: a program that leaves them out, or rounds other values in their place, can miss the bound.
Values may be sent and summed in bfloat16 or wider, within the bound.
A program may use at most 128 MiB of HBM per device.

v0:
```python
import functools
import math
import jax
import jax.numpy as jnp
from jax import lax
from jax.sharding import PartitionSpec as P


def layer_norm_rows(alignment_block):
    content_vectors = alignment_block.astype(jnp.float32)
    centered = content_vectors - jnp.mean(content_vectors, axis=-1, keepdims=True)
    inverse_deviation = lax.rsqrt(jnp.mean(centered * centered, axis=-1, keepdims=True) + 1e-05)
    return (centered * inverse_deviation, inverse_deviation)


def row_backward(bias_full, head_count, dbias_total, row_inputs):
    probe_vectors, keys_row, values_row, gate_row, derivative_modulated = row_inputs
    query_total, channel_width = probe_vectors.shape
    key_count = keys_row.shape[0]
    head_width = channel_width // head_count
    softmax_scale = 1.0 / math.sqrt(head_width)
    query_heads = probe_vectors.reshape(query_total, head_count, head_width)
    key_heads = keys_row.reshape(key_count, head_count, head_width)
    value_heads = values_row.reshape(key_count, head_count, head_width)
    scores = (
        jnp.einsum("ihd,jhd->hij", query_heads, key_heads, preferred_element_type=jnp.float32)
        * softmax_scale
    )
    scores = scores + bias_full.astype(jnp.float32)
    weights_soft = jax.nn.softmax(scores, axis=-1)
    weights_half = weights_soft.astype(jnp.bfloat16)
    attended = jnp.einsum(
        "hij,jhd->ihd", weights_half, value_heads, preferred_element_type=jnp.float32
    ).reshape(query_total, channel_width)
    modulated_result = (gate_row * attended).astype(jnp.bfloat16)
    grad_attended = (derivative_modulated * gate_row).astype(jnp.bfloat16)
    derivative_logits_sigmoid = (
        derivative_modulated * attended * gate_row * (1.0 - gate_row)
    ).astype(jnp.bfloat16)
    grad_heads = grad_attended.reshape(query_total, head_count, head_width)
    grad_weights = jnp.einsum(
        "ihd,jhd->hij", grad_heads, value_heads, preferred_element_type=jnp.float32
    )
    row_inner = jnp.sum(weights_soft * grad_weights, axis=-1, keepdims=True)
    grad_scores = weights_soft * (grad_weights - row_inner)
    scores_half = grad_scores.astype(jnp.bfloat16)
    derivative_probe_weights = (
        jnp.einsum("hij,jhd->ihd", scores_half, key_heads, preferred_element_type=jnp.float32)
        * softmax_scale
    ).astype(jnp.bfloat16)
    derivative_lookup_weights = (
        jnp.einsum("hij,ihd->jhd", scores_half, query_heads, preferred_element_type=jnp.float32)
        * softmax_scale
    )
    derivative_content_weights = jnp.einsum(
        "hij,ihd->jhd", weights_half, grad_heads, preferred_element_type=jnp.float32
    )
    outputs = (
        modulated_result,
        derivative_logits_sigmoid,
        derivative_probe_weights.reshape(query_total, channel_width),
        derivative_lookup_weights.reshape(key_count, channel_width),
        derivative_content_weights.reshape(key_count, channel_width),
    )
    return (dbias_total + grad_scores, outputs)


def body(
    homolog_embedding,
    pair_input_rows,
    incoming_slope,
    rescale_factor,
    probe_weights,
    lookup_weights,
    content_weights,
    sigmoid_weights,
    final_projection,
    pair_bias_matrix,
):
    highest = lax.Precision.HIGHEST
    head_count = pair_bias_matrix.shape[1]
    row_total, query_total, channel_width = homolog_embedding.shape
    standardized_rows, inverse_deviation = layer_norm_rows(homolog_embedding)
    rescaled_embedding = (standardized_rows * rescale_factor).astype(jnp.bfloat16)
    rescaled_plain = rescaled_embedding.reshape(-1, channel_width)
    probe_vectors = (
        jnp.dot(rescaled_plain, probe_weights, preferred_element_type=jnp.float32)
        .astype(jnp.bfloat16)
        .reshape(row_total, query_total, channel_width)
    )
    sigmoid_factors = jax.nn.sigmoid(
        jnp.dot(rescaled_plain, sigmoid_weights, preferred_element_type=jnp.float32)
    ).reshape(row_total, query_total, channel_width)
    incoming_slope_plain = incoming_slope.reshape(-1, channel_width)
    derivative_modulated = jnp.dot(
        incoming_slope_plain, final_projection.T, preferred_element_type=jnp.float32
    ).reshape(row_total, query_total, channel_width)
    bias_local = jnp.einsum(
        "ijc,ch->hij", pair_input_rows, pair_bias_matrix, preferred_element_type=jnp.float32
    ).astype(jnp.bfloat16)
    bias_full = lax.all_gather(bias_local, "seq", axis=2, tiled=True)
    normed_all = lax.all_gather(rescaled_embedding, "res", axis=1, tiled=True)
    key_count = normed_all.shape[1]
    all_flat = normed_all.reshape(-1, channel_width)
    lookup_vectors = (
        jnp.dot(all_flat, lookup_weights, preferred_element_type=jnp.float32)
        .astype(jnp.bfloat16)
        .reshape(row_total, key_count, channel_width)
    )
    content_vectors = (
        jnp.dot(all_flat, content_weights, preferred_element_type=jnp.float32)
        .astype(jnp.bfloat16)
        .reshape(row_total, key_count, channel_width)
    )
    dbias_init = jnp.zeros(bias_full.shape, jnp.float32)
    dbias_local, row_results = lax.scan(
        functools.partial(row_backward, bias_full, head_count),
        dbias_init,
        (probe_vectors, lookup_vectors, content_vectors, sigmoid_factors, derivative_modulated),
    )
    (
        modulated_result,
        derivative_logits_sigmoid,
        derivative_probe_weights,
        derivative_lookup_weights,
        derivative_content_weights,
    ) = row_results
    key_weight_wide = lookup_weights.astype(jnp.float32)
    value_weight_wide = content_weights.astype(jnp.float32)
    lookup_plain = derivative_lookup_weights.reshape(-1, channel_width)
    content_plain = derivative_content_weights.reshape(-1, channel_width)
    key_term = (
        jnp.dot(lookup_plain, key_weight_wide.T, precision=highest)
        + jnp.dot(content_plain, value_weight_wide.T, precision=highest)
    ).reshape(row_total, -1, channel_width)
    grad_from_keys = lax.psum_scatter(key_term, "res", scatter_dimension=1, tiled=True).reshape(
        -1, channel_width
    )
    all_wide = all_flat.astype(jnp.float32)
    part_key = jnp.dot(all_wide.T, lookup_plain, precision=highest)
    part_value = jnp.dot(all_wide.T, content_plain, precision=highest)
    probe_plain = derivative_probe_weights.reshape(-1, channel_width)
    sigmoid_factor_plain = derivative_logits_sigmoid.reshape(-1, channel_width)
    part_query = jnp.dot(rescaled_plain.T, probe_plain, preferred_element_type=jnp.float32)
    part_gate = jnp.dot(rescaled_plain.T, sigmoid_factor_plain, preferred_element_type=jnp.float32)
    part_out = jnp.dot(
        modulated_result.reshape(-1, channel_width).T,
        incoming_slope_plain,
        preferred_element_type=jnp.float32,
    )
    derivative_rescaled = (
        jnp.dot(probe_plain, probe_weights.T, preferred_element_type=jnp.float32)
        + jnp.dot(sigmoid_factor_plain, sigmoid_weights.T, preferred_element_type=jnp.float32)
        + grad_from_keys
    )
    derivative_rescaled = derivative_rescaled.reshape(row_total, query_total, channel_width)
    part_gain = jnp.sum(derivative_rescaled * standardized_rows, axis=(0, 1))
    centered_scaled_gradient = derivative_rescaled * rescale_factor
    alignment_rows_gradient = (
        inverse_deviation
        * (
            centered_scaled_gradient
            - jnp.mean(centered_scaled_gradient, axis=-1, keepdims=True)
            - standardized_rows
            * jnp.mean(centered_scaled_gradient * standardized_rows, axis=-1, keepdims=True)
        )
    ).astype(jnp.bfloat16)
    dbias_own = lax.psum_scatter(dbias_local, "seq", scatter_dimension=2, tiled=True).astype(
        jnp.bfloat16
    )
    pair_input_gradient = jnp.einsum(
        "hij,ch->ijc", dbias_own, pair_bias_matrix, preferred_element_type=jnp.float32
    ).astype(jnp.bfloat16)
    part_bias = jnp.einsum(
        "ijc,hij->ch", pair_input_rows, dbias_own, preferred_element_type=jnp.float32
    )
    totals = lax.psum(
        (part_gain, part_query, part_key, part_value, part_gate, part_out, part_bias),
        ("seq", "res"),
    )
    return (
        alignment_rows_gradient,
        pair_input_gradient,
        totals[0],
        totals[1],
        totals[2],
        totals[3],
        totals[4],
        totals[5],
        totals[6],
    )


def solution(mesh):
    in_specs = (
        P("seq", "res", None),
        P("res", "seq", None),
        P("seq", "res", None),
        P(),
        P(),
        P(),
        P(),
        P(),
        P(),
        P(),
    )
    out_specs = (P("seq", "res", None), P("res", "seq", None), P(), P(), P(), P(), P(), P(), P())
    return jax.shard_map(body, mesh=mesh, in_specs=in_specs, out_specs=out_specs, check_vma=False)
```

profile of v0, /device:TPU:1, one launch (start us, length us, event | category | flops | bytes accessed | tf_op | source)
XLA Modules:
  0.0 668.8 jit_solution(14989727427753423162)
XLA Ops:
  7.3 6.7 convolution_convert_fusion.3
  18.7 28.2 %all-gather.5.cloned.1.call-done = bf16[8,64,2048]{2,0,1:T(8,128)(2,1)} async-done(((bf16[8,64,512]{2,0,1:T(8,128)(2,1)}), bf16[8,64,2048]{2,0,1:T(8,128)(2,1)}) %all-gather.5.cloned.1.call-update) | async-done | bytes 2097168 | tf_op jit(solution)/shard_map/all_gather | solution.py:101
  46.9 4.1 copy.34
  51.0 80.8 %all-gather.3.cloned.1.call-done = bf16[4,2048,256]{2,1,0:T(8,128)(2,1)} async-done(((bf16[4,64,256]{2,1,0:T(8,128)(2,1)}), bf16[4,2048,256]{2,1,0:T(8,128)(2,1)}) %all-gather.3.cloned.1.call-update) | async-done | bytes 4194320 | tf_op jit(solution)/shard_map/all_gather | solution.py:102
  131.8 5.6 convolution_convert_fusion
  140.6 105.2 %while.21 = (s32[]{:T(128)}, f32[8,64,2048]{2,1,0:T(8,128)}, bf16[4,64,256]{1,2,0:T(8,128)(2,1)}, bf16[4,64,256]{1,2,0:T(8,128)(2,1)}, bf16[4,64,256]{1,2,0:T(8,...) while((s32[]{:T(128)}, f32[8,64,2048]{2,1,0:T(8,128)}, ...), condition=%wide.region_6.7_spmd.clone, body=%wide.region_2.6_spmd.clone.sunk | while | flops 422233600 | bytes 126007688 | solution.py:116
  145.4 4.9 fusion.108
  158.8 3.5 fusion.111
  171.7 4.9 fusion.108
  185.1 3.5 fusion.111
  198.0 4.9 fusion.108
  211.4 3.5 fusion.111
  224.3 4.9 fusion.108
  246.1 8.8 %copy.40 = f32[4,2048,256]{2,1,0:T(8,128)} copy(f32[4,2048,256]{1,2,0:T(8,128)} %get-tuple-element.83) | data formatting | bytes 16777216 | tf_op jit(solution)/shard_map/while | solution.py:116
  254.8 8.7 %copy.41 = f32[4,2048,256]{2,1,0:T(8,128)} copy(f32[4,2048,256]{1,2,0:T(8,128)} %get-tuple-element.84) | data formatting | bytes 16777216 | tf_op jit(solution)/shard_map/while | solution.py:116
  263.6 6.7 %fusion.38 = f32[8192,256]{1,0:T(8,128)S(1)} fusion(f32[8192,256]{1,0:T(8,128)} %bitcast.143, bf16[256,256]{1,0:T(8,128)(2,1)S(1)} %copy-done), kind=kOutput, calls=%fused_computation.79 | convolution fusion | flops 6442450944 | bytes 16908288 | tf_op jit(solution)/shard_map/dot_general | solution.py:133
  270.3 6.4 convolution_add_fusion
  281.1 11.1 %convolution_bitcast_fusion.2 = f32[256,256]{1,0:T(8,128)} fusion(bf16[4,2048,256]{2,1,0:T(8,128)(2,1)} %all-gather.3.cloned.1.call-done, f32[4,2048,256]{1,2,0:T(8,128)} %get-tuple-element.84), kind=kOutput, calls=%fused_computation.40 | convolution fusion | flops 6442450944 | bytes 12845056 | tf_op jit(solution)/shard_map/dot_general | solution.py:141
  292.2 8.4 %convolution_bitcast_fusion.3 = f32[256,256]{1,0:T(8,128)} fusion(bf16[4,2048,256]{2,1,0:T(8,128)(2,1)S(1)} %copy-done.5, f32[4,2048,256]{1,2,0:T(8,128)} %get-tuple-element.83), kind=kOutput, calls=%fused_computation.41 | convolution fusion | flops 6442450944 | bytes 12845056 | tf_op jit(solution)/shard_map/dot_general | solution.py:140
  301.9 4.8 convolution_bitcast_fusion.5
  306.8 5.5 convolution_convert_fusion.2
  312.4 165.3 %reduce-scatter.3.cloned.1.call-done = f32[4,64,256]{2,1,0:T(8,128)} async-done(((f32[4,2048,256]{2,1,0:T(8,128)}), f32[4,64,256]{2,1,0:T(8,128)}) %reduce-scatter.3.cloned.1.call-update) | async-done | bytes 262160 | tf_op jit(solution)/shard_map/reduce_scatter | solution.py:136
  479.2 84.4 %all-reduce = (f32[256]{0:T(256)}, f32[128,8]{0,1:T(8,128)}) all-reduce(f32[256]{0:T(256)S(1)} %get-tuple-element.155, f32[128,8]{0,1:T(8,128)S(1)} %convolution_bitcast_fusion.5), channel_id=1, replica_groups=mesh['seq'=4,'res'=32] {'seq','res'}, use_global_device_ids=true, to_apply=%region_12.13 | all-reduce | flops 1280 | bytes 10240 | tf_op jit(solution)/shard_map/psum | solution.py:177
  564.5 89.4 %all-reduce.4.cloned.1.call-done = (f32[256,256]{1,0:T(8,128)}, f32[256,256]{1,0:T(8,128)}, f32[256,256]{1,0:T(8,128)}, f32[256,256]{1,0:T(8,128)}, f32[256,256]{1,0:T(8,128)}) async-done(((f32[256,256]{1,0:T(8,128)}, f32[256,256]{1,0:T(8,128)}, f32[256,256]{1,0:T(8,128)}, f32[256,256]{1,0:T(8,128)}, f32[256,256]{1,0:T(8,128)}), (f32[256,256]{1,0:T(8,128)}, f32[256,256]{1,0:T(8,128)}, f32[256,256]{1,0:T(8,128)}, ...) | async-done | bytes 1310736 | tf_op jit(solution)/shard_map/psum | solution.py:177
  (221 shorter events, 98.9 us)
Async XLA Ops:
  7.2 130.2 %copy-start = (bf16[256,256]{1,0:T(8,128)(2,1)S(1)}, bf16[256,256]{1,0:T(8,128)(2,1)}, u32[]{:S(2)}) copy-start(bf16[256,256]{1,0:T(8,128)(2,1)} %param.17) | copy-start | bytes 393220
  7.2 6.9 %copy-start.8 = (bf16[4,64,256]{2,1,0:T(8,128)(2,1)S(1)}, bf16[4,64,256]{2,1,0:T(8,128)(2,1)}, u32[]{:S(2)}) copy-start(bf16[4,64,256]{2,1,0:T(8,128)(2,1)} %param.12) | copy-start | bytes 393220
  7.2 7.2 %copy-start.30 = (f32[256]{0:T(256)S(1)}, f32[256]{0:T(256)}, u32[]{:S(2)}) copy-start(f32[256]{0:T(256)} %param.15) | copy-start | bytes 3076
  7.2 8.2 %copy-start.18 = (bf16[256,256]{1,0:T(8,128)(2,1)S(1)}, bf16[256,256]{1,0:T(8,128)(2,1)}, u32[]{:S(2)}) copy-start(bf16[256,256]{1,0:T(8,128)(2,1)} %param.16) | copy-start | bytes 393220
  7.2 9.3 %copy-start.24 = (bf16[256,256]{1,0:T(8,128)(2,1)S(1)}, bf16[256,256]{1,0:T(8,128)(2,1)}, u32[]{:S(2)}) copy-start(bf16[256,256]{1,0:T(8,128)(2,1)} %param.19) | copy-start | bytes 393220
  7.2 10.4 %copy-start.16 = (bf16[4,64,256]{2,1,0:T(8,128)(2,1)S(1)}, bf16[4,64,256]{2,1,0:T(8,128)(2,1)}, u32[]{:S(2)}) copy-start(bf16[4,64,256]{2,1,0:T(8,128)(2,1)} %param.14) | copy-start | bytes 393220
  7.3 10.4 %copy-start.23 = (bf16[256,256]{1,0:T(8,128)(2,1)S(1)}, bf16[256,256]{1,0:T(8,128)(2,1)}, u32[]{:S(2)}) copy-start(bf16[256,256]{1,0:T(8,128)(2,1)} %param.20) | copy-start | bytes 393220
  7.3 39.7 %all-gather.5.cloned.1.call-start = ((), (), s32[]{:S(2)}) async-start(), calls=%async_computation.3 | async-start | bytes 2621440 | tf_op jit(solution)/shard_map/all_gather | solution.py:101
  14.0 117.8 %copy-start.14 = (bf16[256,256]{1,0:T(8,128)(2,1)S(1)}, bf16[256,256]{1,0:T(8,128)(2,1)}, u32[]{:S(2)}) copy-start(bf16[256,256]{1,0:T(8,128)(2,1)} %param.18) | copy-start | bytes 393220
  14.0 117.8 %all-gather.3.cloned.1.call-start = ((), (), s32[]{:S(2)}) async-start(), calls=%async_computation.2 | async-start | bytes 4325376 | tf_op jit(solution)/shard_map/all_gather | solution.py:102
  15.3 285.4 %reduce-scatter.5.cloned.1.call-start = ((), (), s32[]{:S(2)}) async-start(), calls=%async_computation.5 | async-start | bytes 5242880 | tf_op jit(solution)/shard_map/reduce_scatter | solution.py:168
  131.8 5.6 copy-start.4
  229.2 4.7 copy-start.1
  245.8 231.8 %reduce-scatter.3.cloned.1.call-start = ((), (), s32[]{:S(2)}) async-start(), calls=%async_computation.4 | async-start | bytes 8650752 | tf_op jit(solution)/shard_map/reduce_scatter | solution.py:136
  263.6 6.7 %copy-start.6 = (f32[4,2048,256]{2,1,0:T(8,128)S(1)}, f32[4,2048,256]{2,1,0:T(8,128)}, u32[]{:S(2)}) copy-start(f32[4,2048,256]{2,1,0:T(8,128)} %copy.41) | copy-start | bytes 25165828
  263.6 6.7 %copy-start.15 = (bf16[256,256]{1,0:T(8,128)(2,1)S(1)}, bf16[256,256]{1,0:T(8,128)(2,1)}, u32[]{:S(2)}) copy-start(bf16[256,256]{1,0:T(8,128)(2,1)} %param.18) | copy-start | bytes 393220
  276.8 377.2 %all-reduce.4.cloned.1.call-start = ((), (), s32[]{:S(2)}) async-start(), calls=%async_computation.6 | async-start | bytes 2621440 | tf_op jit(solution)/shard_map/psum | solution.py:177
  281.1 11.1 %copy-start.5 = (bf16[4,2048,256]{2,1,0:T(8,128)(2,1)S(1)}, bf16[4,2048,256]{2,1,0:T(8,128)(2,1)}, u32[]{:S(2)}) copy-start(bf16[4,2048,256]{2,1,0:T(8,128)(2,1)} %all-gather.3.cloned.1.call-done) | copy-start | bytes 12582916
  301.9 4.8 copy-start.32
  306.8 170.9 %copy-start.25 = (bf16[256,256]{1,0:T(8,128)(2,1)S(1)}, bf16[256,256]{1,0:T(8,128)(2,1)}, u32[]{:S(2)}) copy-start(bf16[256,256]{1,0:T(8,128)(2,1)} %param.19) | copy-start | bytes 393220
  306.8 170.9 %copy-start.31 = (f32[256]{0:T(256)S(1)}, f32[256]{0:T(256)}, u32[]{:S(2)}) copy-start(f32[256]{0:T(256)} %param.15) | copy-start | bytes 3076
  306.8 172.2 %copy-start.9 = (bf16[4,64,256]{2,1,0:T(8,128)(2,1)S(1)}, bf16[4,64,256]{2,1,0:T(8,128)(2,1)}, u32[]{:S(2)}) copy-start(bf16[4,64,256]{2,1,0:T(8,128)(2,1)} %param.12) | copy-start | bytes 393220
  306.8 172.2 %copy-start.27 = (f32[4,64]{1,0:T(4,128)S(1)}, f32[4,64]{1,0:T(4,128)}, u32[]{:S(2)}) copy-start(f32[4,64]{1,0:T(4,128)} %copy-done.26) | copy-start | bytes 3076
  306.8 172.2 %copy-start.29 = (f32[4,64]{1,0:T(4,128)S(1)}, f32[4,64]{1,0:T(4,128)}, u32[]{:S(2)}) copy-start(f32[4,64]{1,0:T(4,128)} %copy-done.28) | copy-start | bytes 3076
  (35 other events, 85.4 us)
Sparse Core Ops, SparseCore 0:
  14.1 32.7 all-gather.4
  50.6 81.1 all-gather.2
  246.0 44.0 reduce-scatter.4
  292.3 185.3 reduce-scatter.2
  483.8 170.0 all-reduce.3
where the time goes:
time: 670 us; the launch traced here: 669 us
  waiting for transfers between devices  364 us (54%)
  matrix products  116 us (17%)
  blocking collectives  84.4 us (13%)
  local copies, waits for them, and re-layouts  68.2 us (10%)
  other arithmetic  21.5 us (3%)
  between operations  14.2 us (2%)
    reduce_scatter x1, waiting for transfers between devices, body(): lax.psum_scatter(key_term, 'res', scatter_dimension=1, tiled=True)  165 us
    psum x1, waiting for transfers between devices, body(): lax.psum((part_gain, part_query, part_key, part_value, part_gate, part_ou...  89.4 us
    psum x1, blocking collectives, body(): lax.psum((part_gain, part_query, part_key, part_value, part_gate, part_ou...  84.4 us
    all_gather x1, waiting for transfers between devices, body(): normed_all = lax.all_gather(rescaled_embedding, 'res', axis=1, tiled=True)  80.8 us
    all_gather x1, waiting for transfers between devices, body(): bias_full = lax.all_gather(bias_local, 'seq', axis=2, tiled=True)  28.2 us
    sub x4, matrix products, row_backward(): weights_soft = jax.nn.softmax(scores, axis=-1)  19.8 us
    while x4, local copies, waits for them, and re-layouts, body(): lax.scan(functools.partial(row_backward, bias_full, head_count), dbias_in...  17.7 us
    dynamic_slice x32, local copies, waits for them, and re-layouts, body(): lax.scan(functools.partial(row_backward, bias_full, head_count), dbias_in...  16.4 us
  transfers between devices with their start and end apart: 5, of which 4 were waited for; matrix products, arithmetic and copies ran while one was open for 11% of the time, Pallas kernels for 0%

commit v1 on v0

--- a/solution.py
+++ b/solution.py
@@ -99,7 +99,7 @@
         "ijc,ch->hij", pair_input_rows, pair_bias_matrix, preferred_element_type=jnp.float32
     ).astype(jnp.bfloat16)
     bias_full = lax.all_gather(bias_local, "seq", axis=2, tiled=True)
-    normed_all = lax.all_gather(rescaled_embedding, "res", axis=1, tiled=True)
+    normed_all = jnp.concatenate(lax.all_gather(rescaled_embedding, "res"), axis=1)
     key_count = normed_all.shape[1]
     all_flat = normed_all.reshape(-1, channel_width)
     lookup_vectors = (

time: 670 us -> 709 us (1.058)
  waiting for transfers between devices: 364 us -> 379 us
  local copies, waits for them, and re-layouts: 68.2 us -> 80.7 us
  matrix products: 116 us -> 126 us
    dynamic_update_slice x12 -> x20, local copies, waits for them, and re-layouts: 16.3 us -> 40.4 us  [body(): lax.scan(functools.partial(row_backward, bias_full, head_count), dbias_in...]
    while x4 -> x2, local copies, waits for them, and re-layouts: 17.7 us -> 0.25 us  [body(): lax.scan(functools.partial(row_backward, bias_full, head_count), dbias_in...]
    dot_general x4, matrix products: 11 us -> 22.1 us  [row_backward(): jnp.einsum('ihd,jhd->hij', grad_heads, value_heads, preferred_element_typ...]
    reduce_scatter x1, waiting for transfers between devices: 165 us -> 176 us  [body(): lax.psum_scatter(key_term, 'res', scatter_dimension=1, tiled=True)]
  transfers between devices with their start and end apart: 5 -> 5, of which waited for: 4 -> 5; matrix products, arithmetic and copies ran while one was open for 11% -> 8% of each run, Pallas kernels for 0% -> 0%
where the time goes in v1:
time: 709 us; the launch traced here: 708 us
  waiting for transfers between devices  379 us (53%)
  matrix products  126 us (18%)
  blocking collectives  84.9 us (12%)
  local copies, waits for them, and re-layouts  80.7 us (11%)
  other arithmetic  21.5 us (3%)
  between operations  14.2 us (2%)
    reduce_scatter x1, waiting for transfers between devices, body(): lax.psum_scatter(key_term, 'res', scatter_dimension=1, tiled=True)  176 us
    psum x1, waiting for transfers between devices, body(): lax.psum((part_gain, part_query, part_key, part_value, part_gate, part_ou...  88.9 us
    psum x1, blocking collectives, body(): lax.psum((part_gain, part_query, part_key, part_value, part_gate, part_ou...  84.9 us
    all_gather x1, waiting for transfers between devices, body(): lax.all_gather(rescaled_embedding, 'res')  80.5 us
    dynamic_update_slice x20, local copies, waits for them, and re-layouts, body(): lax.scan(functools.partial(row_backward, bias_full, head_count), dbias_in...  40.4 us
    all_gather x1, waiting for transfers between devices, body(): bias_full = lax.all_gather(bias_local, 'seq', axis=2, tiled=True)  28.2 us
    dot_general x4, matrix products, row_backward(): jnp.einsum('ihd,jhd->hij', grad_heads, value_heads, preferred_element_typ...  22.1 us
    sub x4, matrix products, row_backward(): weights_soft = jax.nn.softmax(scores, axis=-1)  20 us
  transfers between devices with their start and end apart: 5, of which 5 were waited for; matrix products, arithmetic and copies ran while one was open for 8% of the time, Pallas kernels for 0%

profile of v1, /device:TPU:1, one launch (start us, length us, event | category | flops | bytes accessed | tf_op | source)
XLA Modules:
  0.0 707.6 jit_solution(18113908633212325826)
XLA Ops:
  7.3 6.7 convolution_convert_fusion.3
  18.7 28.2 %all-gather.4.cloned.1.call-done = bf16[8,64,2048]{2,0,1:T(8,128)(2,1)} async-done(((bf16[8,64,512]{2,0,1:T(8,128)(2,1)}), bf16[8,64,2048]{2,0,1:T(8,128)(2,1)}) %all-gather.4.cloned.1.call-update) | async-done | bytes 2097168 | tf_op jit(solution)/shard_map/all_gather | solution.py:101
  51.0 80.5 %all-gather.6.cloned.1.call-done = bf16[128,64,256]{2,1,0:T(8,128)(2,1)} async-done(((bf16[4,64,256]{2,1,0:T(8,128)(2,1)}), bf16[128,64,256]{2,1,0:T(8,128)(2,1)}) %all-gather.6.cloned.1.call-update) | async-done | bytes 4194320 | tf_op jit(solution)/shard_map/all_gather | solution.py:102
  140.5 143.9 %while.21 = (s32[]{:T(128)}, f32[8,64,2048]{2,1,0:T(8,128)}, bf16[4,64,256]{1,2,0:T(8,128)(2,1)}, bf16[4,64,256]{1,2,0:T(8,128)(2,1)}, bf16[4,64,256]{1,2,0:T(8,...) while((s32[]{:T(128)}, f32[8,64,2048]{2,1,0:T(8,128)}, ...), condition=%wide.region_6.7_spmd.clone, body=%wide.region_2.6_spmd.clone.sunk | while | flops 422233600 | bytes 155630096 | solution.py:116
  145.7 5.0 fusion.110
  157.8 5.5 multiply_reduce_fusion.3
  171.9 4.6 constant_dynamic-update-slice_fusion.10
  181.6 5.0 fusion.110
  193.7 5.5 multiply_reduce_fusion.3
  217.6 5.0 fusion.110
  229.7 5.5 multiply_reduce_fusion.3
  243.9 4.6 constant_dynamic-update-slice_fusion.10
  253.6 5.0 fusion.110
  265.7 5.5 multiply_reduce_fusion.3
  284.7 6.7 fusion.38
  291.4 6.4 convolution_add_fusion
  303.1 11.3 %fusion.40 = f32[256,256]{1,0:T(8,128)} fusion(bf16[8192,256]{1,0:T(8,128)(2,1)} %bitcast.142, f32[8192,256]{1,0:T(8,128)} %bitcast.148), kind=kOutput, calls=%fused_computation.79 | convolution fusion | flops 6442450944 | bytes 12845056 | tf_op jit(solution)/shard_map/dot_general | solution.py:141
  314.4 8.7 %fusion.39 = f32[256,256]{1,0:T(8,128)} fusion(bf16[8192,256]{1,0:T(8,128)(2,1)S(1)} %bitcast.143, f32[8192,256]{1,0:T(8,128)} %bitcast.145), kind=kOutput, calls=%fused_computation.78 | convolution fusion | flops 6442450944 | bytes 12845056 | tf_op jit(solution)/shard_map/dot_general | solution.py:140
  323.2 5.6 reduce-scatter.5.cloned.1.call-done
  330.0 4.8 convolution_bitcast_fusion.3
  334.9 5.5 convolution_convert_fusion.2
  340.4 176.0 %reduce-scatter.3.cloned.1.call-done = f32[4,64,256]{2,1,0:T(8,128)} async-done(((f32[4,2048,256]{2,1,0:T(8,128)}), f32[4,64,256]{2,1,0:T(8,128)}) %reduce-scatter.3.cloned.1.call-update) | async-done | bytes 262160 | tf_op jit(solution)/shard_map/reduce_scatter | solution.py:136
  518.1 84.9 %all-reduce = (f32[256]{0:T(256)}, f32[128,8]{0,1:T(8,128)}) all-reduce(f32[256]{0:T(256)S(1)} %get-tuple-element.181, f32[128,8]{0,1:T(8,128)S(1)} %convolution_bitcast_fusion.3), channel_id=1, replica_groups=mesh['seq'=4,'res'=32] {'seq','res'}, use_global_device_ids=true, to_apply=%region_12.13 | all-reduce | flops 1280 | bytes 10240 | tf_op jit(solution)/shard_map/psum | solution.py:177
  603.8 88.9 %all-reduce.4.cloned.1.call-done = (f32[256,256]{1,0:T(8,128)}, f32[256,256]{1,0:T(8,128)}, f32[256,256]{1,0:T(8,128)}, f32[256,256]{1,0:T(8,128)}, f32[256,256]{1,0:T(8,128)}) async-done(((f32[256,256]{1,0:T(8,128)}, f32[256,256]{1,0:T(8,128)}, f32[256,256]{1,0:T(8,128)}, f32[256,256]{1,0:T(8,128)}, f32[256,256]{1,0:T(8,128)}), (f32[256,256]{1,0:T(8,128)}, f32[256,256]{1,0:T(8,128)}, f32[256,256]{1,0:T(8,128)}, ...) | async-done | bytes 1310736 | tf_op jit(solution)/shard_map/psum | solution.py:177
  (261 shorter events, 127.5 us)
Async XLA Ops:
  7.2 130.1 %copy-start = (bf16[256,256]{1,0:T(8,128)(2,1)S(1)}, bf16[256,256]{1,0:T(8,128)(2,1)}, u32[]{:S(2)}) copy-start(bf16[256,256]{1,0:T(8,128)(2,1)} %param.17) | copy-start | bytes 393220
  7.2 6.9 copy-start.9
  7.2 7.2 %copy-start.32 = (f32[256]{0:T(256)S(1)}, f32[256]{0:T(256)}, u32[]{:S(2)}) copy-start(f32[256]{0:T(256)} %param.15) | copy-start | bytes 3076
  7.2 8.2 %copy-start.21 = (bf16[256,256]{1,0:T(8,128)(2,1)S(1)}, bf16[256,256]{1,0:T(8,128)(2,1)}, u32[]{:S(2)}) copy-start(bf16[256,256]{1,0:T(8,128)(2,1)} %param.16) | copy-start | bytes 393220
  7.2 9.3 %copy-start.26 = (bf16[256,256]{1,0:T(8,128)(2,1)S(1)}, bf16[256,256]{1,0:T(8,128)(2,1)}, u32[]{:S(2)}) copy-start(bf16[256,256]{1,0:T(8,128)(2,1)} %param.19) | copy-start | bytes 393220
  7.2 10.4 %copy-start.19 = (bf16[4,64,256]{2,1,0:T(8,128)(2,1)S(1)}, bf16[4,64,256]{2,1,0:T(8,128)(2,1)}, u32[]{:S(2)}) copy-start(bf16[4,64,256]{2,1,0:T(8,128)(2,1)} %param.14) | copy-start | bytes 393220
  7.3 10.4 %copy-start.25 = (bf16[256,256]{1,0:T(8,128)(2,1)S(1)}, bf16[256,256]{1,0:T(8,128)(2,1)}, u32[]{:S(2)}) copy-start(bf16[256,256]{1,0:T(8,128)(2,1)} %param.20) | copy-start | bytes 393220
  7.3 39.7 %all-gather.4.cloned.1.call-start = ((), (), s32[]{:S(2)}) async-start(), calls=%async_computation.2 | async-start | bytes 2621440 | tf_op jit(solution)/shard_map/all_gather | solution.py:101
  14.0 117.5 %all-gather.6.cloned.1.call-start = ((), (), s32[]{:S(2)}) async-start(), calls=%async_computation.5 | async-start | bytes 4325376 | tf_op jit(solution)/shard_map/all_gather | solution.py:102
  15.3 313.5 %reduce-scatter.5.cloned.1.call-start = ((), (), s32[]{:S(2)}) async-start(), calls=%async_computation.4 | async-start | bytes 5242880 | tf_op jit(solution)/shard_map/reduce_scatter | solution.py:168
  143.3 7.3 %copy-start.7 = (bf16[1,2048,256]{1,2,0:T(8,128)(2,1)}, bf16[1,2048,256]{1,2,0:T(8,128)(2,1)S(1)}, u32[]{:S(2)}) copy-start(bf16[1,2048,256]{1,2,0:T(8,128)(2,1)S(1)} %copy.107) | copy-start | bytes 3145732 | tf_op jit(solution)/shard_map/while
  179.3 7.3 %copy-start.7 = (bf16[1,2048,256]{1,2,0:T(8,128)(2,1)}, bf16[1,2048,256]{1,2,0:T(8,128)(2,1)S(1)}, u32[]{:S(2)}) copy-start(bf16[1,2048,256]{1,2,0:T(8,128)(2,1)S(1)} %copy.107) | copy-start | bytes 3145732 | tf_op jit(solution)/shard_map/while
  215.3 7.3 %copy-start.7 = (bf16[1,2048,256]{1,2,0:T(8,128)(2,1)}, bf16[1,2048,256]{1,2,0:T(8,128)(2,1)S(1)}, u32[]{:S(2)}) copy-start(bf16[1,2048,256]{1,2,0:T(8,128)(2,1)S(1)} %copy.107) | copy-start | bytes 3145732 | tf_op jit(solution)/shard_map/while
  251.2 7.3 %copy-start.7 = (bf16[1,2048,256]{1,2,0:T(8,128)(2,1)}, bf16[1,2048,256]{1,2,0:T(8,128)(2,1)S(1)}, u32[]{:S(2)}) copy-start(bf16[1,2048,256]{1,2,0:T(8,128)(2,1)S(1)} %copy.107) | copy-start | bytes 3145732 | tf_op jit(solution)/shard_map/while
  284.5 232.0 %reduce-scatter.3.cloned.1.call-start = ((), (), s32[]{:S(2)}) async-start(), calls=%async_computation.3 | async-start | bytes 8650752 | tf_op jit(solution)/shard_map/reduce_scatter | solution.py:136
  284.7 6.7 slice-start
  284.7 6.7 slice-start.1
  297.8 394.9 %all-reduce.4.cloned.1.call-start = ((), (), s32[]{:S(2)}) async-start(), calls=%async_computation.6 | async-start | bytes 2621440 | tf_op jit(solution)/shard_map/psum | solution.py:177
  303.1 11.3 %copy-start.6 = (bf16[4,32,64,256]{3,2,1,0:T(8,128)(2,1)S(1)}, bf16[4,32,64,256]{3,2,1,0:T(8,128)(2,1)}, u32[]{:S(2)}) copy-start(bf16[4,32,64,256]{3,2,1,0:T(8,128)(2,1)} %copy-done.5) | copy-start | bytes 12582916
  334.9 181.6 %copy-start.27 = (bf16[256,256]{1,0:T(8,128)(2,1)S(1)}, bf16[256,256]{1,0:T(8,128)(2,1)}, u32[]{:S(2)}) copy-start(bf16[256,256]{1,0:T(8,128)(2,1)} %param.19) | copy-start | bytes 393220
  334.9 181.6 %copy-start.33 = (f32[256]{0:T(256)S(1)}, f32[256]{0:T(256)}, u32[]{:S(2)}) copy-start(f32[256]{0:T(256)} %param.15) | copy-start | bytes 3076
  334.9 183.0 %copy-start.10 = (bf16[4,64,256]{2,1,0:T(8,128)(2,1)S(1)}, bf16[4,64,256]{2,1,0:T(8,128)(2,1)}, u32[]{:S(2)}) copy-start(bf16[4,64,256]{2,1,0:T(8,128)(2,1)} %param.12) | copy-start | bytes 393220
  334.9 183.0 %copy-start.29 = (f32[4,64]{1,0:T(4,128)S(1)}, f32[4,64]{1,0:T(4,128)}, u32[]{:S(2)}) copy-start(f32[4,64]{1,0:T(4,128)} %copy-done.28) | copy-start | bytes 3076
  334.9 182.9 %copy-start.31 = (f32[4,64]{1,0:T(4,128)S(1)}, f32[4,64]{1,0:T(4,128)}, u32[]{:S(2)}) copy-start(f32[4,64]{1,0:T(4,128)} %copy-done.30) | copy-start | bytes 3076
  (51 other events, 161.2 us)
Sparse Core Ops, SparseCore 0:
  14.1 32.7 all-gather.3
  50.5 80.9 all-gather.5
  284.6 44.0 reduce-scatter.4
  331.0 185.4 reduce-scatter.2
  522.6 170.0 all-reduce.3
